TPU v7x, 128 devices: a whole 4x4x4 slice. The times are simulated.
128 devices in a mesh: row: 8 (over z, core), col: 16 (over y, x).
Axes of the slice: x: 4, y: 4, z: 4, core: 2. Of those that a mesh axis runs over, the one named last changes fastest.
Arguments:
- front_diag: float32 [1024, 1024], replicated, may hold values from -4 to 16, as said below
- panel_rows: float32 [16384, 1024], P(('row', 'col')), may hold values from -1.2 to 1.2
- trailing: float32 [16384, 16384], P('row', 'col'), may hold values from -6 to 6
- pattern: int32 [64, 64], P('row', 'col'), may hold values 0 or 1
Outputs:
- diag_factor: float32 [1024, 1024], replicated
- panel_factor: float32 [16384, 1024], P(('row', 'col'))
- schur: float32 [16384, 16384], P('row', 'col')
Inputs may be any that keep to these rules, and one draw needn't show every extreme that they name: front_diag is symmetric and positive definite, with smallest eigenvalue at least 0.5.
All inputs are finite; a program needn't handle non-finite values. No bound on the sum of `pattern` on one device may be relied on, other than what follows from the above.
Results may differ from a plain program's by a relative error of at most 0.0003.
Values sent between devices are 32-bit elements; how exact they have to be, the bound alone decides.
A program may use at most 128 MiB of HBM per device.

v0:
```python
import jax
import jax.numpy as jnp
from jax import lax
from jax.sharding import PartitionSpec as P

BLOCK = 256


def spread(block, axis, holder):
    block = jnp.where(lax.axis_index(axis) == holder, block, jnp.zeros_like(block))
    return lax.psum(block, axis)


def column_rows(row_part, col_rows):
    ratio = lax.axis_size("col") // lax.axis_size("row")
    offset = lax.axis_index("col") % ratio * col_rows
    return lax.dynamic_slice_in_dim(row_part, offset, col_rows, 0)


def local(front_diag, panel_rows, trailing, pattern):
    diag_factor = jnp.linalg.cholesky(front_diag)
    panel_factor = jax.scipy.linalg.solve_triangular(diag_factor, panel_rows.T, lower=True).T
    local_rows = trailing.shape[0]
    col_rows = trailing.shape[1]
    ratio = lax.axis_size("col") // lax.axis_size("row")
    root_row = lax.axis_index("col") // ratio
    row_part = lax.all_gather(panel_factor, "col", axis=0, tiled=True)
    piece = column_rows(row_part, col_rows)
    col_part = spread(piece, "row", root_row)
    update = jnp.dot(row_part, col_part.T, precision=lax.Precision.HIGHEST)
    row_blocks = local_rows // BLOCK
    col_blocks = col_rows // BLOCK
    row_index = lax.axis_index("row") * row_blocks + jnp.arange(row_blocks)
    col_index = lax.axis_index("col") * col_blocks + jnp.arange(col_blocks)
    lower = (row_index[:, None] >= col_index[None, :]).astype(jnp.float32)
    keep = pattern.astype(jnp.float32) * lower
    masked = update.reshape(row_blocks, BLOCK, col_blocks, BLOCK) * keep[:, None, :, None]
    schur = trailing - masked.reshape(local_rows, col_rows)
    return (diag_factor, panel_factor, schur)


def solution(mesh):
    return jax.shard_map(
        local,
        mesh=mesh,
        in_specs=(P(), P(("row", "col"), None), P("row", "col"), P("row", "col")),
        out_specs=(P(), P(("row", "col"), None), P("row", "col")),
        check_vma=False,
    )
```

profile of v0, /device:TPU:0, one launch (start us, length us, event | category | flops | bytes accessed | tf_op | source)
XLA Modules:
  0.0 537.7 jit_solution(12177218288238149050)
XLA Ops:
  7.2 5.3 copy.7
  12.6 4.4 fusion
  17.0 2.0 copy-done
  19.0 11.7 %cholesky.223 = f32[128,128]{1,0:T(8,128)S(1)} custom-call(f32[128,128]{1,0:T(8,128)S(1)} %cholesky.580), custom_call_target="Cholesky" | custom-call | tf_op jit(solution)/shard_map/jit(cholesky)/cholesky | solution.py:21
  30.8 9.8 %custom-call.63 = f32[1,128,128]{1,2,0:T(8,128)S(1)} custom-call(f32[1,128,128]{2,1,0:T(8,128)S(1)} %get-tuple-element.61), custom_call_target="InvertDiagBlocksLowerTriangular" | custom-call | tf_op jit(solution)/shard_map/jit(cholesky)/cholesky | solution.py:21
  40.6 2.5 cholesky.255
  43.1 2.3 constant_dynamic-update-slice_fusion.32
  45.4 1.5 convolution_subtract_fusion
  47.0 11.9 %cholesky.244 = f32[128,128]{1,0:T(8,128)S(1)} custom-call(f32[128,128]{1,0:T(8,128)S(1)} %cholesky.584), custom_call_target="Cholesky" | custom-call | tf_op jit(solution)/shard_map/jit(cholesky)/cholesky | solution.py:21
  59.5 9.8 %custom-call.64 = f32[1,128,128]{1,2,0:T(8,128)S(1)} custom-call(f32[1,128,128]{2,1,0:T(8,128)S(1)} %get-tuple-element.58), custom_call_target="InvertDiagBlocksLowerTriangular" | custom-call | tf_op jit(solution)/shard_map/jit(cholesky)/cholesky | solution.py:21
  70.5 2.1 convolution_subtract_fusion.1
  72.7 11.7 %cholesky.468 = f32[128,128]{1,0:T(8,128)S(1)} custom-call(f32[128,128]{1,0:T(8,128)S(1)} %cholesky.589), custom_call_target="Cholesky" | custom-call | tf_op jit(solution)/shard_map/jit(cholesky)/cholesky | solution.py:21
  85.7 9.8 %custom-call.65 = f32[1,128,128]{1,2,0:T(8,128)S(1)} custom-call(f32[1,128,128]{2,1,0:T(8,128)S(1)} %get-tuple-element.55), custom_call_target="InvertDiagBlocksLowerTriangular" | custom-call | tf_op jit(solution)/shard_map/jit(cholesky)/cholesky | solution.py:21
  96.6 2.3 convolution_subtract_fusion.2
  99.0 11.9 %cholesky.487 = f32[128,128]{1,0:T(8,128)S(1)} custom-call(f32[128,128]{1,0:T(8,128)S(1)} %cholesky.594), custom_call_target="Cholesky" | custom-call | tf_op jit(solution)/shard_map/jit(cholesky)/cholesky | solution.py:21
  112.2 9.8 %custom-call.66 = f32[1,128,128]{1,2,0:T(8,128)S(1)} custom-call(f32[1,128,128]{2,1,0:T(8,128)S(1)} %get-tuple-element.52), custom_call_target="InvertDiagBlocksLowerTriangular" | custom-call | tf_op jit(solution)/shard_map/jit(cholesky)/cholesky | solution.py:21
  123.1 2.4 convolution_subtract_fusion.3
  125.4 11.7 %cholesky.506 = f32[128,128]{1,0:T(8,128)S(1)} custom-call(f32[128,128]{1,0:T(8,128)S(1)} %cholesky.599), custom_call_target="Cholesky" | custom-call | tf_op jit(solution)/shard_map/jit(cholesky)/cholesky | solution.py:21
  138.5 10.2 %custom-call.67 = f32[1,128,128]{1,2,0:T(8,128)S(1)} custom-call(f32[1,128,128]{2,1,0:T(8,128)S(1)} %get-tuple-element.49), custom_call_target="InvertDiagBlocksLowerTriangular" | custom-call | tf_op jit(solution)/shard_map/jit(cholesky)/cholesky | solution.py:21
  149.7 2.3 convolution_subtract_fusion.4
  152.0 11.7 %cholesky.526 = f32[128,128]{1,0:T(8,128)S(1)} custom-call(f32[128,128]{1,0:T(8,128)S(1)} %cholesky.604), custom_call_target="Cholesky" | custom-call | tf_op jit(solution)/shard_map/jit(cholesky)/cholesky | solution.py:21
  165.0 9.8 %custom-call.68 = f32[1,128,128]{1,2,0:T(8,128)S(1)} custom-call(f32[1,128,128]{2,1,0:T(8,128)S(1)} %get-tuple-element.46), custom_call_target="InvertDiagBlocksLowerTriangular" | custom-call | tf_op jit(solution)/shard_map/jit(cholesky)/cholesky | solution.py:21
  175.8 2.1 convolution_subtract_fusion.5
  177.9 11.9 %cholesky.546 = f32[128,128]{1,0:T(8,128)S(1)} custom-call(f32[128,128]{1,0:T(8,128)S(1)} %cholesky.609), custom_call_target="Cholesky" | custom-call | tf_op jit(solution)/shard_map/jit(cholesky)/cholesky | solution.py:21
  191.0 9.8 %custom-call.69 = f32[1,128,128]{1,2,0:T(8,128)S(1)} custom-call(f32[1,128,128]{2,1,0:T(8,128)S(1)} %get-tuple-element.43), custom_call_target="InvertDiagBlocksLowerTriangular" | custom-call | tf_op jit(solution)/shard_map/jit(cholesky)/cholesky | solution.py:21
  201.7 1.8 convolution_subtract_fusion.11
  203.4 11.7 %cholesky.564 = f32[128,128]{1,0:T(8,128)S(1)} custom-call(f32[128,128]{1,0:T(8,128)S(1)} %convolution_subtract_fusion.11), custom_call_target="Cholesky" | custom-call | tf_op jit(solution)/shard_map/jit(cholesky)/cholesky | solution.py:21
  222.0 6.8 %fusion.1 = (f32[1024,1024]{1,0:T(8,128)}, f32[1024,1024]{1,0:T(8,128)}) fusion(f32[1024,1024]{1,0:T(8,128)} %get-tuple-element.41, pred[]{:T(512)S(6)} %cholesky.579), kind=kLoop, calls=%fused_computation.8 | loop fusion | flops 4194304 | bytes 12582913 | tf_op jit(solution)/shard_map/jit(_solve_triangular)/triangular_solve | solution.py:22
  228.8 22.5 %while.1 = (s32[]{:T(128)}, f32[1024,1024]{1,0:T(8,128)}, s32[8,2]{0,1:T(2,128)S(1)}, f32[8,128,128]{2,1,0:T(8,128)S(1)}, s32[]{:T(128)}) while((s32[]{:T(128)}, f32[1024,1024]{1,0:T(8,128)}, s32[8,2]{0,1:T(2,128)S(1)}, f32[8,128,128]{2,1,0:T(8,128)S(1)}, s32[]{:T(128)}) %tuple.58), condition=%wide.while_cond, body=%wide.while_body.sunk | while | flops 2 | bytes 131189 | solution.py:22
  229.4 2.2 bitcast_dynamic-update-slice_fusion.2
  232.3 2.2 bitcast_dynamic-update-slice_fusion.2
  235.1 2.2 bitcast_dynamic-update-slice_fusion.2
  237.9 2.2 bitcast_dynamic-update-slice_fusion.2
  240.7 2.2 bitcast_dynamic-update-slice_fusion.2
  243.5 2.2 bitcast_dynamic-update-slice_fusion.2
  246.4 2.2 bitcast_dynamic-update-slice_fusion.2
  249.2 2.1 bitcast_dynamic-update-slice_fusion.2
  251.3 78.8 %custom-call.70 = f32[8,128,128]{1,2,0:T(8,128)S(1)} custom-call(f32[8,128,128]{2,1,0:T(8,128)S(1)} %get-tuple-element.10), custom_call_target="InvertDiagBlocksLowerTriangular" | custom-call | tf_op jit(solution)/shard_map/jit(_solve_triangular)/triangular_solve | solution.py:22
  333.8 1.4 convolution_subtract_fusion.13
  335.5 1.5 convolution_subtract_fusion.12
  337.4 1.7 convolution_subtract_fusion.8
  339.4 1.8 convolution_subtract_fusion.7
  341.5 1.9 convolution_subtract_fusion.6
  344.9 73.2 %all-gather.2.cloned.1.call-done = f32[2048,1024]{1,0:T(8,128)} async-done(((f32[128,1024]{1,0:T(8,128)}), f32[2048,1024]{1,0:T(8,128)}) %all-gather.2.cloned.1.call-update) | async-done | bytes 8388624 | tf_op jit(solution)/shard_map/all_gather | solution.py:27
  418.1 5.0 dynamic-slice_select_fusion
  425.0 5.5 %copy.18 = f32[256,8,4,256]{3,1,2,0:T(8,128)} copy(f32[256,8,4,256]{3,2,1,0:T(4,128)S(1)} %bitcast.109) | data formatting | bytes 16777216
  430.5 65.2 %all-reduce.3.cloned.1.call-done = f32[1024,1024]{1,0:T(8,128)} async-done(((f32[1024,1024]{1,0:T(8,128)}), f32[1024,1024]{1,0:T(8,128)}) %all-reduce.3.cloned.1.call-update) | async-done | bytes 4194320 | tf_op jit(solution)/shard_map/psum | solution.py:11
  495.8 34.7 %multiply_subtract_fusion = f32[2048,1024]{1,0:T(8,128)} fusion(f32[2048,1024]{1,0:T(8,128)} %param.6, f32[2048,1024]{1,0:T(8,128)} %bitcast.108, f32[2048,1024]{1,0:T(8,128)} %all-gather.2.cloned.1.call-done, f32[1024,1024]{1,0:T(8,128)} %all-reduce.3.cloned.1.call-done), kind=kOutput, calls=%fused_computation.2 | convolution fusion | flops 25773998080 | bytes 37748736 | tf_op jit(solution)/shard_map/dot_general | solution.py:30
  (87 shorter events, 28.2 us)
Async XLA Ops:
  7.2 410.9 %all-gather.2.cloned.1.call-start = ((), (), s32[]{:S(2)}) async-start(), calls=%async_computation | async-start | bytes 8912896 | tf_op jit(solution)/shard_map/all_gather | solution.py:27
  17.0 2.0 copy-start
  222.0 108.2 %copy-start.2 = (f32[128,1024]{1,0:T(8,128)S(1)}, f32[128,1024]{1,0:T(8,128)}, u32[]{:S(2)}) copy-start(f32[128,1024]{1,0:T(8,128)} %param.5) | copy-start | bytes 1572868
  344.0 0.8 copy-start.1
  344.8 150.9 %all-reduce.3.cloned.1.call-start = ((), (), s32[]{:S(2)}) async-start(), calls=%async_computation.1 | async-start | bytes 8388608 | tf_op jit(solution)/shard_map/psum | solution.py:11
  423.1 0.7 copy-start.3
Sparse Core Ops, SparseCore 0:
  345.0 73.0 all-gather.1
  423.2 72.5 all-reduce.2
where the time goes:
time: 548 us; the launch traced here: 538 us
  other arithmetic  267 us (49%)
  waiting for transfers between devices  138 us (25%)
  matrix products  70.7 us (13%)
  local copies, waits for them, and re-layouts  41.1 us (8%)
  between operations  19.9 us (4%)
    another operation x30, other arithmetic, local(): diag_factor = jnp.linalg.cholesky(front_diag)  172 us
    another operation x3, other arithmetic, local(): jax.scipy.linalg.solve_triangular(diag_factor, panel_rows.T, lower=True)  85.7 us
    all_gather x1, waiting for transfers between devices, local(): row_part = lax.all_gather(panel_factor, 'col', axis=0, tiled=True)  73.2 us
    psum x1, waiting for transfers between devices, spread(): return lax.psum(block, axis)  65.2 us
    dot_general x1, matrix products, local(): update = jnp.dot(row_part, col_part.T, precision=lax.Precision.HIGHEST)  34.7 us
    another operation x14, matrix products, local(): diag_factor = jnp.linalg.cholesky(front_diag)  23 us
    another operation x24, local copies, waits for them, and re-layouts  22.4 us
    unnamed x17, local copies, waits for them, and re-layouts  14.3 us
  transfers between devices with their start and end apart: 2, of which 2 were waited for; matrix products, arithmetic and copies ran while one was open for 1% of the time, Pallas kernels for 0%

commit v1 on v0

--- a/solution.py
+++ b/solution.py
@@ -24,7 +24,9 @@
     col_rows = trailing.shape[1]
     ratio = lax.axis_size("col") // lax.axis_size("row")
     root_row = lax.axis_index("col") // ratio
-    row_part = lax.all_gather(panel_factor, "col", axis=0, tiled=True)
+    row_part = jnp.concatenate(
+        lax.all_to_all(jnp.stack([panel_factor] * lax.axis_size("col")), "col", 0, 0), axis=0
+    )
     piece = column_rows(row_part, col_rows)
     col_part = spread(piece, "row", root_row)
     update = jnp.dot(row_part, col_part.T, precision=lax.Precision.HIGHEST)

time: 548 us -> 651 us (1.19)
  waiting for transfers between devices: 138 us -> 188 us
  local copies, waits for them, and re-layouts: 41.1 us -> 77.7 us
  other arithmetic: 267 us -> 279 us
  starting transfers between devices: 0.08 us -> 7.22 us
    all_to_all x0 -> x1, waiting for transfers between devices: none -> 124 us  [local(): lax.all_to_all(jnp.stack([panel_factor] * lax.axis_size('col')), 'col', 0...]
    all_gather x1 -> x0, waiting for transfers between devices: 73.2 us -> none  [local(): row_part = lax.all_gather(panel_factor, 'col', axis=0, tiled=True)]
    unnamed x17 -> x13, local copies, waits for them, and re-layouts: 14.3 us -> 37.5 us
    sub x0 -> x1, other arithmetic: none -> 11.7 us  [local(): schur = trailing - masked.reshape(local_rows, col_rows)]
    mul x1, local copies, waits for them, and re-layouts: 1.15 us -> 10.7 us  [local(): update.reshape(row_blocks, BLOCK, col_blocks, BLOCK)]
    all_to_all x0 -> x1, starting transfers between devices: none -> 7.17 us  [local(): lax.all_to_all(jnp.stack([panel_factor] * lax.axis_size('col')), 'col', 0...]
    another operation x24 -> x25, local copies, waits for them, and re-layouts: 22.4 us -> 26.8 us
where the time goes in v1:
time: 651 us; the launch traced here: 641 us
  other arithmetic  279 us (43%)
  waiting for transfers between devices  188 us (29%)
  local copies, waits for them, and re-layouts  77.7 us (12%)
  matrix products  68.6 us (11%)
  between operations  19.8 us (3%)
  starting transfers between devices  7.22 us (1%)
    another operation x30, other arithmetic, local(): diag_factor = jnp.linalg.cholesky(front_diag)  172 us
    all_to_all x1, waiting for transfers between devices, local(): lax.all_to_all(jnp.stack([panel_factor] * lax.axis_size('col')), 'col', 0...  124 us
    another operation x3, other arithmetic, local(): jax.scipy.linalg.solve_triangular(diag_factor, panel_rows.T, lower=True)  85.7 us
    psum x1, waiting for transfers between devices, spread(): return lax.psum(block, axis)  64 us
    unnamed x13, local copies, waits for them, and re-layouts  37.5 us
    dot_general x1, matrix products, local(): update = jnp.dot(row_part, col_part.T, precision=lax.Precision.HIGHEST)  32.5 us
    another operation x14, matrix products, local(): diag_factor = jnp.linalg.cholesky(front_diag)  23 us
    another operation x24, local copies, waits for them, and re-layouts  22.4 us
  transfers between devices with their start and end apart: 2, of which 2 were waited for; matrix products, arithmetic and copies ran while one was open for 1% of the time, Pallas kernels for 0%

profile of v1, /device:TPU:0, one launch (start us, length us, event | category | flops | bytes accessed | tf_op | source)
XLA Modules:
  0.0 640.5 jit_solution(1181591148166487707)
XLA Ops:
  7.2 5.3 copy.11
  12.5 4.4 fusion.2
  17.0 2.0 copy-done
  19.0 11.7 %cholesky.223 = f32[128,128]{1,0:T(8,128)S(1)} custom-call(f32[128,128]{1,0:T(8,128)S(1)} %cholesky.580), custom_call_target="Cholesky" | custom-call | tf_op jit(solution)/shard_map/jit(cholesky)/cholesky | solution.py:21
  30.7 9.8 %custom-call.63 = f32[1,128,128]{1,2,0:T(8,128)S(1)} custom-call(f32[1,128,128]{2,1,0:T(8,128)S(1)} %get-tuple-element.75), custom_call_target="InvertDiagBlocksLowerTriangular" | custom-call | tf_op jit(solution)/shard_map/jit(cholesky)/cholesky | solution.py:21
  40.6 2.5 cholesky.255
  43.1 2.3 constant_dynamic-update-slice_fusion.32
  47.0 11.9 %cholesky.244 = f32[128,128]{1,0:T(8,128)S(1)} custom-call(f32[128,128]{1,0:T(8,128)S(1)} %cholesky.584), custom_call_target="Cholesky" | custom-call | tf_op jit(solution)/shard_map/jit(cholesky)/cholesky | solution.py:21
  59.5 9.8 %custom-call.64 = f32[1,128,128]{1,2,0:T(8,128)S(1)} custom-call(f32[1,128,128]{2,1,0:T(8,128)S(1)} %get-tuple-element.72), custom_call_target="InvertDiagBlocksLowerTriangular" | custom-call | tf_op jit(solution)/shard_map/jit(cholesky)/cholesky | solution.py:21
  70.5 2.1 convolution_subtract_fusion.1
  72.6 11.7 %cholesky.468 = f32[128,128]{1,0:T(8,128)S(1)} custom-call(f32[128,128]{1,0:T(8,128)S(1)} %cholesky.589), custom_call_target="Cholesky" | custom-call | tf_op jit(solution)/shard_map/jit(cholesky)/cholesky | solution.py:21
  85.6 9.8 %custom-call.65 = f32[1,128,128]{1,2,0:T(8,128)S(1)} custom-call(f32[1,128,128]{2,1,0:T(8,128)S(1)} %get-tuple-element.69), custom_call_target="InvertDiagBlocksLowerTriangular" | custom-call | tf_op jit(solution)/shard_map/jit(cholesky)/cholesky | solution.py:21
  96.6 2.3 convolution_subtract_fusion.2
  98.9 11.9 %cholesky.487 = f32[128,128]{1,0:T(8,128)S(1)} custom-call(f32[128,128]{1,0:T(8,128)S(1)} %cholesky.594), custom_call_target="Cholesky" | custom-call | tf_op jit(solution)/shard_map/jit(cholesky)/cholesky | solution.py:21
  112.1 9.8 %custom-call.66 = f32[1,128,128]{1,2,0:T(8,128)S(1)} custom-call(f32[1,128,128]{2,1,0:T(8,128)S(1)} %get-tuple-element.66), custom_call_target="InvertDiagBlocksLowerTriangular" | custom-call | tf_op jit(solution)/shard_map/jit(cholesky)/cholesky | solution.py:21
  123.0 2.4 convolution_subtract_fusion.3
  125.4 11.7 %cholesky.506 = f32[128,128]{1,0:T(8,128)S(1)} custom-call(f32[128,128]{1,0:T(8,128)S(1)} %cholesky.599), custom_call_target="Cholesky" | custom-call | tf_op jit(solution)/shard_map/jit(cholesky)/cholesky | solution.py:21
  138.4 10.2 %custom-call.67 = f32[1,128,128]{1,2,0:T(8,128)S(1)} custom-call(f32[1,128,128]{2,1,0:T(8,128)S(1)} %get-tuple-element.63), custom_call_target="InvertDiagBlocksLowerTriangular" | custom-call | tf_op jit(solution)/shard_map/jit(cholesky)/cholesky | solution.py:21
  149.6 2.3 convolution_subtract_fusion.4
  152.0 11.7 %cholesky.526 = f32[128,128]{1,0:T(8,128)S(1)} custom-call(f32[128,128]{1,0:T(8,128)S(1)} %cholesky.604), custom_call_target="Cholesky" | custom-call | tf_op jit(solution)/shard_map/jit(cholesky)/cholesky | solution.py:21
  165.0 9.8 %custom-call.68 = f32[1,128,128]{1,2,0:T(8,128)S(1)} custom-call(f32[1,128,128]{2,1,0:T(8,128)S(1)} %get-tuple-element.60), custom_call_target="InvertDiagBlocksLowerTriangular" | custom-call | tf_op jit(solution)/shard_map/jit(cholesky)/cholesky | solution.py:21
  175.7 2.1 convolution_subtract_fusion.5
  177.8 11.9 %cholesky.546 = f32[128,128]{1,0:T(8,128)S(1)} custom-call(f32[128,128]{1,0:T(8,128)S(1)} %cholesky.609), custom_call_target="Cholesky" | custom-call | tf_op jit(solution)/shard_map/jit(cholesky)/cholesky | solution.py:21
  191.0 9.8 %custom-call.69 = f32[1,128,128]{1,2,0:T(8,128)S(1)} custom-call(f32[1,128,128]{2,1,0:T(8,128)S(1)} %get-tuple-element.57), custom_call_target="InvertDiagBlocksLowerTriangular" | custom-call | tf_op jit(solution)/shard_map/jit(cholesky)/cholesky | solution.py:21
  203.4 11.7 %cholesky.564 = f32[128,128]{1,0:T(8,128)S(1)} custom-call(f32[128,128]{1,0:T(8,128)S(1)} %convolution_subtract_fusion.11), custom_call_target="Cholesky" | custom-call | tf_op jit(solution)/shard_map/jit(cholesky)/cholesky | solution.py:21
  221.9 6.8 %fusion.3 = (f32[1024,1024]{1,0:T(8,128)}, f32[1024,1024]{1,0:T(8,128)}) fusion(f32[1024,1024]{1,0:T(8,128)} %get-tuple-element.55, pred[]{:T(512)S(6)} %cholesky.579), kind=kLoop, calls=%fused_computation.10 | loop fusion | flops 4194304 | bytes 12582913 | tf_op jit(solution)/shard_map/jit(_solve_triangular)/triangular_solve | solution.py:22
  228.8 22.5 %while.1 = (s32[]{:T(128)}, f32[1024,1024]{1,0:T(8,128)}, s32[8,2]{0,1:T(2,128)S(1)}, f32[8,128,128]{2,1,0:T(8,128)S(1)}, s32[]{:T(128)}) while((s32[]{:T(128)}, f32[1024,1024]{1,0:T(8,128)}, s32[8,2]{0,1:T(2,128)S(1)}, f32[8,128,128]{2,1,0:T(8,128)S(1)}, s32[]{:T(128)}) %tuple.64), condition=%wide.while_cond, body=%wide.while_body.sunk | while | flops 2 | bytes 131189 | solution.py:22
  229.4 2.2 bitcast_dynamic-update-slice_fusion.2
  232.2 2.2 bitcast_dynamic-update-slice_fusion.2
  235.0 2.2 bitcast_dynamic-update-slice_fusion.2
  237.8 2.2 bitcast_dynamic-update-slice_fusion.2
  240.7 2.2 bitcast_dynamic-update-slice_fusion.2
  243.5 2.2 bitcast_dynamic-update-slice_fusion.2
  246.3 2.2 bitcast_dynamic-update-slice_fusion.2
  249.1 2.1 bitcast_dynamic-update-slice_fusion.2
  251.3 78.8 %custom-call.70 = f32[8,128,128]{1,2,0:T(8,128)S(1)} custom-call(f32[8,128,128]{2,1,0:T(8,128)S(1)} %get-tuple-element.10), custom_call_target="InvertDiagBlocksLowerTriangular" | custom-call | tf_op jit(solution)/shard_map/jit(_solve_triangular)/triangular_solve | solution.py:22
  341.1 1.9 convolution_subtract_fusion.6
  343.5 4.5 stack.2
  348.0 7.2 %all-to-all-start = ((f32[16,128,1024]{2,1,0:T(8,128)}), f32[16,128,1024]{2,1,0:T(8,128)}, u32[]{:S(2)}, u32[]{:S(2)}) async-start(f32[16,128,1024]{2,1,0:T(8,128)} %stack.2), calls=%async_computation | async-start | bytes 16777216 | tf_op jit(solution)/shard_map/all_to_all | solution.py:28
  355.3 123.9 %all-to-all-done = f32[16,128,1024]{2,1,0:T(8,128)} async-done(((f32[16,128,1024]{2,1,0:T(8,128)}), f32[16,128,1024]{2,1,0:T(8,128)}, u32[]{:S(2)}, u32[]{:S(2)}) %all-to-all-start) | async-done | bytes 8388640 | tf_op jit(solution)/shard_map/all_to_all | solution.py:28
  479.2 5.0 dynamic-slice_select_fusion
  485.1 9.4 %copy.15 = f32[2048,1024]{0,1:T(8,128)} copy(f32[2048,1024]{1,0:T(8,128)} %param.6) | data formatting | bytes 16777216 | tf_op args[2]
  494.4 64.0 %all-reduce.3.cloned.1.call-done = f32[4,256,1024]{2,1,0:T(8,128)} async-done(((f32[4,256,1024]{2,1,0:T(8,128)}), f32[4,256,1024]{2,1,0:T(8,128)}) %all-reduce.3.cloned.1.call-update) | async-done | bytes 4194320 | tf_op jit(solution)/shard_map/psum | solution.py:11
  558.4 32.5 %broadcast_multiply_fusion = f32[8,256,4,256]{3,1,2,0:T(8,128)} fusion(f32[8,4]{1,0:T(8,128)S(1)} %copy.13, f32[8,256,1024,1]{2,1,3,0:T(8,128)} %bitcast.27, f32[4,256,1024]{2,1,0:T(8,128)} %all-reduce.3.cloned.1.call-done), kind=kOutput, calls=%fused_computation.6 | convolution fusion | flops 25771900928 | bytes 20971648 | tf_op jit(solution)/shard_map/dot_general | solution.py:32
  590.9 10.7 %copy.14 = f32[8,256,4,256]{1,0,3,2:T(8,128)} copy(f32[8,256,4,256]{3,1,2,0:T(8,128)} %broadcast_multiply_fusion) | data formatting | bytes 16777216 | tf_op jit(solution)/shard_map/mul | solution.py:39
  601.5 10.7 %copy.19 = f32[128,8,8,256]{3,1,2,0:T(8,128)} copy(f32[128,8,8,256]{3,2,1,0:T(8,128)} %bitcast.122) | data formatting | bytes 16777216
  612.2 11.7 %sub.8 = f32[2048,1024]{0,1:T(8,128)} subtract(f32[2048,1024]{0,1:T(8,128)} %copy.15, f32[2048,1024]{0,1:T(8,128)} %bitcast.121) | non-fusion elementwise | flops 2097152 | bytes 25165824 | tf_op jit(solution)/shard_map/sub | solution.py:40
  623.9 9.2 %copy.17 = f32[2048,1024]{1,0:T(8,128)} copy(f32[2048,1024]{0,1:T(8,128)} %sub.8) | data formatting | bytes 16777216
  (77 shorter events, 35.6 us)
Async XLA Ops:
  17.0 2.0 copy-start
  221.9 108.2 %copy-start.2 = (f32[128,1024]{1,0:T(8,128)S(1)}, f32[128,1024]{1,0:T(8,128)}, u32[]{:S(2)}) copy-start(f32[128,1024]{1,0:T(8,128)} %param.5) | copy-start | bytes 1572868
  343.5 4.5 copy-start.1
  348.0 131.2 %all-to-all-start = ((f32[16,128,1024]{2,1,0:T(8,128)}), f32[16,128,1024]{2,1,0:T(8,128)}, u32[]{:S(2)}, u32[]{:S(2)}) async-start(f32[16,128,1024]{2,1,0:T(8,128)} %stack.2), calls=%async_computation | async-start | bytes 16777216 | tf_op jit(solution)/shard_map/all_to_all | solution.py:28
  355.2 203.1 %all-reduce.3.cloned.1.call-start = ((), (), s32[]{:S(2)}) async-start(), calls=%async_computation.1 | async-start | bytes 8388608 | tf_op jit(solution)/shard_map/psum | solution.py:11
  484.2 0.7 copy-start.3
Sparse Core Ops, SparseCore 0:
  484.4 73.9 all-reduce.2
